TPU v7x, 32 devices: a whole 2x2x4 slice. The times are simulated.
32 devices in a mesh: arc: 8 (over z, core), col: 4 (over y, x).
Axes of the slice: x: 2, y: 2, z: 4, core: 2. Of those that a mesh axis runs over, the one named last changes fastest.
Arguments:
- design: bfloat16 [12288, 5120], P('arc', 'col'), may hold values from -0.109375 to 0.109375
- local_design: float32 [16, 12288], P(None, 'arc'), may hold values from -6 to 6
- observed: float32 [12288], P('arc'), may hold values from -6 to 6
- valid_mask: int32 [12288], P('arc'), may hold values 0 or 1
- counts: int32 [64], P('arc'), may hold values from 1 to 192, 7680 in all
Outputs:
- normal: float32 [5120, 5120], P('arc', 'col')
- rhs: float32 [5120], P('col')
Inputs may be any that keep to these rules, and one draw needn't show every extreme that they name: Arc a holds counts[a] recorded slots at its start; the rest are padding.
All inputs are finite; a program needn't handle non-finite values. No bound on the sum of `valid_mask` or of `counts` on one device may be relied on, other than what follows from the above.
Results may differ from a plain program's by a relative error of at most 0.0028.
Values may be sent and summed in bfloat16 or wider, within the bound.
A program may use at most 128 MiB of HBM per device.

v0:
```python
import jax
import jax.numpy as jnp
from jax import lax
from jax.sharding import PartitionSpec as P


def eliminate(block_design, block_local, block_observed, block_live):
    highest = lax.Precision.HIGHEST
    masked = block_local * block_live[None, :]
    gram_matrix = jnp.dot(masked, block_local.T, precision=highest) + jnp.eye(
        block_local.shape[0], dtype=jnp.float32
    )
    factor = jnp.linalg.cholesky(gram_matrix)
    inverse = jax.scipy.linalg.cho_solve(
        (factor, True), jnp.eye(block_local.shape[0], dtype=jnp.float32)
    )
    dense = block_design.astype(jnp.float32)
    cross_terms = jnp.dot(masked, dense, precision=highest)
    cross_obs = jnp.dot(masked, block_observed, precision=highest)
    projector = jnp.dot(inverse, cross_terms, precision=highest)
    projected = block_live[:, None] * (dense - jnp.dot(block_local.T, projector, precision=highest))
    solved_obs = jnp.dot(inverse, cross_obs, precision=highest)
    residual = block_live * (block_observed - jnp.dot(block_local.T, solved_obs, precision=highest))
    return (projected.astype(jnp.bfloat16), residual)


def column_product(column_piece, projected):
    return lax.dot_general(
        column_piece, projected, (((0,), (0,)), ((), ())), preferred_element_type=jnp.float32
    )


def shards(design, local_design, observed, valid_mask, counts):
    row_count, col_width = design.shape
    arc_count = counts.shape[0]
    slot_count = row_count // arc_count
    local_count = local_design.shape[0]
    inside = jnp.arange(slot_count, dtype=jnp.int32)[None, :] < counts[:, None]
    live_mask = inside.reshape(-1).astype(jnp.float32) * valid_mask.astype(jnp.float32)
    blocks_local = local_design.reshape(local_count, arc_count, slot_count).transpose(1, 0, 2)
    projected, residual = jax.vmap(eliminate)(
        design.reshape(arc_count, slot_count, col_width),
        blocks_local,
        observed.reshape(arc_count, slot_count),
        live_mask.reshape(arc_count, slot_count),
    )
    projected = projected.reshape(row_count, col_width)
    rhs_part = jnp.dot(
        residual.reshape(row_count), projected.astype(jnp.float32), precision=lax.Precision.HIGHEST
    )
    gathered = lax.all_gather(projected, "col", axis=1, tiled=True)
    normal = lax.psum_scatter(
        column_product(gathered, projected), "arc", scatter_dimension=0, tiled=True
    )
    rhs = lax.psum(rhs_part, "arc")
    return (normal, rhs)


def solution(mesh):
    placed = (P("arc", "col"), P(None, "arc"), P("arc"), P("arc"), P("arc"))
    return jax.shard_map(
        shards, mesh=mesh, in_specs=placed, out_specs=(P("arc", "col"), P("col")), check_vma=False
    )
```

profile of v0, /device:TPU:0, one launch (start us, length us, event | category | flops | bytes accessed | tf_op | source)
XLA Modules:
  0.0 489.1 jit_solution(5814584548888950459)
XLA Ops:
  7.2 0.0 all-gather.2.cloned.1.call-start
  7.2 0.7 iota_compare_fusion.3
  8.0 0.1 lt.20
  8.1 0.7 convert_select_fusion
  8.8 0.1 mul.28
  8.8 1.0 reshape.48
  9.8 0.3 fusion.5
  10.1 0.1 copy.12
  10.2 11.7 %custom-call.11 = f32[8,16,16]{2,1,0:T(8,128)S(1)} custom-call(f32[8,16,16]{2,1,0:T(8,128)S(1)} %fusion.24), custom_call_target="Cholesky" | custom-call | tf_op jit(solution)/shard_map/vmap(jit(cholesky))/cholesky | solution.py:13
  22.0 0.1 compare_reduce_fusion
  22.1 0.1 select_bitcast_fusion
  22.2 9.8 %custom-call.12 = f32[8,1,16,16]{2,3,1,0:T(8,128)S(1)} custom-call(f32[8,1,16,16]{3,2,1,0:T(8,128)S(1)} %select_bitcast_fusion), custom_call_target="InvertDiagBlocksLowerTriangular" | custom-call | tf_op jit(solution)/shard_map/vmap(jit(_cho_solve))/triangular_solve | solution.py:14
  32.0 0.0 copy-start
  32.0 0.4 fusion.21
  32.4 0.2 fusion.19
  32.6 4.0 fusion.8
  36.7 0.7 fusion.34
  37.3 0.0 copy-done
  37.3 8.3 %fusion.1 = bf16[8,192,1280]{2,1,0:T(8,128)(2,1)} fusion(bf16[8,192,1280]{2,1,0:T(8,128)(2,1)S(1)} %bitcast.70, f32[8,16,1280]{2,1,0:T(8,128)S(1)} %fusion.34, f32[8,192]{1,0:T(8,128)S(1)} %mul.28, f32[16,8,192]{2,1,0:T(8,128)S(1)} %reshape.48), kind=kOutput, calls=%fused_computation.2 | convolution fusion | flops 385351680 | bytes 8624128 | tf_op jit(solution)/shard_map/vmap()/dot_general | solution.py:21
  45.6 0.0 all-gather.2.cloned.1.call-update
  45.6 0.2 reduce-scatter.2.cloned.1.call-start
  45.8 151.2 %all-gather.2.cloned.1.call-done = bf16[1536,5120]{1,0:T(8,128)(2,1)} async-done(((bf16[1536,1280]{1,0:T(8,128)(2,1)}), bf16[1536,5120]{1,0:T(8,128)(2,1)}) %all-gather.2.cloned.1.call-update) | async-done | bytes 15728656 | tf_op jit(solution)/shard_map/all_gather | solution.py:51
  197.1 27.5 %fusion.35 = f32[5120,1280]{1,0:T(8,128)} fusion(bf16[1536,5120]{1,0:T(8,128)(2,1)} %all-gather.2.cloned.1.call-done, bf16[1536,1280]{1,0:T(8,128)(2,1)} %bitcast.68), kind=kOutput, calls=%fused_computation.49 | convolution fusion | flops 20132659200 | bytes 45875200 | tf_op jit(solution)/shard_map/dot_general | solution.py:28
  224.5 0.0 copy-start.1
  224.5 0.0 reduce-scatter.2.cloned.1.call-update
  224.6 0.7 copy-done.1
  225.2 0.1 reshape.60
  225.3 0.1 reshape.50
  225.4 0.3 convolution_bitcast_fusion.1
  225.7 0.2 convolution_bitcast_fusion
  225.9 0.2 fusion.2
  226.1 3.8 convolution_reduce_fusion
  229.9 18.2 %psum.7 = f32[1280]{0:T(1024)} all-reduce(f32[1280]{0:T(1024)S(1)} %convolution_reduce_fusion), channel_id=1, replica_groups=mesh['arc'=8,'col'=4] {'arc'}, use_global_device_ids=true, to_apply=%region_3.4 | all-reduce | flops 1280 | bytes 10240 | tf_op jit(solution)/shard_map/psum | solution.py:55
  248.2 234.1 %reduce-scatter.2.cloned.1.call-done = f32[640,1280]{1,0:T(8,128)} async-done(((f32[5120,1280]{1,0:T(8,128)}), f32[640,1280]{1,0:T(8,128)}) %reduce-scatter.2.cloned.1.call-update) | async-done | bytes 3276816 | tf_op jit(solution)/shard_map/reduce_scatter | solution.py:52
  (6 shorter events, 0.1 us)
Async XLA Ops:
  7.2 189.9 %all-gather.2.cloned.1.call-start = ((), (), s32[]{:S(2)}) async-start(), calls=%async_computation.1 | async-start | bytes 19660800 | tf_op jit(solution)/shard_map/all_gather | solution.py:51
  32.0 5.3 %copy-start = (bf16[1536,1280]{1,0:T(8,128)(2,1)S(1)}, bf16[1536,1280]{1,0:T(8,128)(2,1)}, u32[]{:S(2)}) copy-start(bf16[1536,1280]{1,0:T(8,128)(2,1)} %param.5) | copy-start | bytes 11796484
  45.6 436.6 %reduce-scatter.2.cloned.1.call-start = ((), (), s32[]{:S(2)}) async-start(), calls=%async_computation.2 | async-start | bytes 29491200 | tf_op jit(solution)/shard_map/reduce_scatter | solution.py:52
  224.5 0.7 copy-start.1
Sparse Core Ops, SparseCore 0:
  45.7 151.2 all-gather.1
  224.7 257.5 reduce-scatter.1
where the time goes:
time: 489 us
  waiting for transfers between devices  385 us (79%)
  matrix products  45.8 us (9%)
  other arithmetic  23.3 us (5%)
  blocking collectives  18.2 us (4%)
  between operations  14.2 us (3%)
    reduce_scatter x1, waiting for transfers between devices, shards(): lax.psum_scatter(column_product(gathered, projected), 'arc', scatter_dime...  234 us
    all_gather x1, waiting for transfers between devices, shards(): gathered = lax.all_gather(projected, 'col', axis=1, tiled=True)  151 us
    dot_general x1, matrix products, column_product(): lax.dot_general(column_piece, projected, (((0,), (0,)), ((), ())), prefer...  27.5 us
    psum x1, blocking collectives, shards(): rhs = lax.psum(rhs_part, 'arc')  18.2 us
    another operation x4, other arithmetic, eliminate(): factor = jnp.linalg.cholesky(gram_matrix)  11.9 us
    another operation x3, other arithmetic, eliminate(): jax.scipy.linalg.cho_solve((factor, True), jnp.eye(block_local.shape[0],...  9.94 us
  transfers between devices with their start and end apart: 2, of which 2 were waited for; matrix products, arithmetic and copies ran while one was open for 1% of the time, Pallas kernels for 0%

commit v1 on v0

--- a/solution.py
+++ b/solution.py
@@ -48,7 +48,7 @@
     rhs_part = jnp.dot(
         residual.reshape(row_count), projected.astype(jnp.float32), precision=lax.Precision.HIGHEST
     )
-    gathered = lax.all_gather(projected, "col", axis=1, tiled=True)
+    gathered = jnp.concatenate(lax.all_gather(projected, "col"), axis=1)
     normal = lax.psum_scatter(
         column_product(gathered, projected), "arc", scatter_dimension=0, tiled=True
     )

time: 489 us -> 510 us (1.043)
  local copies, waits for them, and re-layouts: 2.05 us -> 22.7 us
    all_gather x0 -> x1, local copies, waits for them, and re-layouts: none -> 20.6 us  [shards(): gathered = jnp.concatenate(lax.all_gather(projected, 'col'), axis=1)]
where the time goes in v1:
time: 510 us; the launch traced here: 509 us
  waiting for transfers between devices  385 us (75%)
  matrix products  45.4 us (9%)
  other arithmetic  23.3 us (5%)
  local copies, waits for them, and re-layouts  22.7 us (4%)
  blocking collectives  18.2 us (4%)
  between operations  14.2 us (3%)
    reduce_scatter x1, waiting for transfers between devices, shards(): lax.psum_scatter(column_product(gathered, projected), 'arc', scatter_dime...  234 us
    all_gather x1, waiting for transfers between devices, shards(): gathered = jnp.concatenate(lax.all_gather(projected, 'col'), axis=1)  151 us
    dot_general x1, matrix products, column_product(): lax.dot_general(column_piece, projected, (((0,), (0,)), ((), ())), prefer...  27.2 us
    all_gather x1, local copies, waits for them, and re-layouts, shards(): gathered = jnp.concatenate(lax.all_gather(projected, 'col'), axis=1)  20.6 us
    psum x1, blocking collectives, shards(): rhs = lax.psum(rhs_part, 'arc')  18.2 us
    another operation x4, other arithmetic, eliminate(): factor = jnp.linalg.cholesky(gram_matrix)  11.9 us
  transfers between devices with their start and end apart: 2, of which 2 were waited for; matrix products, arithmetic and copies ran while one was open for 1% of the time, Pallas kernels for 0%

profile of v1, /device:TPU:0, one launch (start us, length us, event | category | flops | bytes accessed | tf_op | source)
XLA Modules:
  0.0 509.4 jit_solution(10087815201870254478)
XLA Ops:
  7.2 0.0 all-gather.2.cloned.1.call-start
  7.2 0.7 iota_compare_fusion.3
  8.0 0.1 lt.20
  8.1 0.7 convert_select_fusion
  8.8 0.1 mul.28
  8.8 1.0 reshape.54
  9.8 0.3 fusion.5
  10.1 0.1 copy.21
  10.2 11.7 %custom-call.11 = f32[8,16,16]{2,1,0:T(8,128)S(1)} custom-call(f32[8,16,16]{2,1,0:T(8,128)S(1)} %fusion.24), custom_call_target="Cholesky" | custom-call | tf_op jit(solution)/shard_map/vmap(jit(cholesky))/cholesky | solution.py:13
  22.0 0.1 compare_reduce_fusion
  22.1 0.1 select_bitcast_fusion
  22.2 9.8 %custom-call.12 = f32[8,1,16,16]{2,3,1,0:T(8,128)S(1)} custom-call(f32[8,1,16,16]{3,2,1,0:T(8,128)S(1)} %select_bitcast_fusion), custom_call_target="InvertDiagBlocksLowerTriangular" | custom-call | tf_op jit(solution)/shard_map/vmap(jit(_cho_solve))/triangular_solve | solution.py:14
  32.0 0.0 copy-start
  32.0 0.4 fusion.21
  32.4 0.2 fusion.19
  32.6 4.0 fusion.8
  36.6 0.7 fusion.34
  37.3 0.0 copy-done
  37.3 8.2 %fusion.1 = bf16[8,192,1280]{2,1,0:T(8,128)(2,1)} fusion(bf16[8,192,1280]{2,1,0:T(8,128)(2,1)S(1)} %bitcast.74, f32[8,16,1280]{2,1,0:T(8,128)S(1)} %fusion.34, f32[8,192]{1,0:T(8,128)S(1)} %mul.28, f32[16,8,192]{2,1,0:T(8,128)S(1)} %reshape.54), kind=kOutput, calls=%fused_computation.2 | convolution fusion | flops 385351680 | bytes 8624128 | tf_op jit(solution)/shard_map/vmap()/dot_general | solution.py:21
  45.5 0.0 all-gather.2.cloned.1.call-update
  45.6 0.2 reduce-scatter.2.cloned.1.call-start
  45.8 151.2 %all-gather.2.cloned.1.call-done = bf16[4,1536,1280]{2,1,0:T(8,128)(2,1)} async-done(((bf16[1,1536,1280]{2,1,0:T(8,128)(2,1)}), bf16[4,1536,1280]{2,1,0:T(8,128)(2,1)}) %all-gather.2.cloned.1.call-update) | async-done | bytes 15728656 | tf_op jit(solution)/shard_map/all_gather | solution.py:51
  197.0 20.6 %copy.23 = bf16[4,1536,1280]{1,2,0:T(8,128)(2,1)} copy(bf16[4,1536,1280]{2,1,0:T(8,128)(2,1)} %all-gather.2.cloned.1.call-done) | data formatting | bytes 31457280 | tf_op jit(solution)/shard_map/all_gather | solution.py:51
  217.7 27.2 %fusion.35 = f32[5120,1280]{1,0:T(8,128)} fusion(bf16[1536,5120]{0,1:T(8,128)(2,1)} %bitcast.75, bf16[1536,1280]{1,0:T(8,128)(2,1)} %bitcast.72), kind=kOutput, calls=%fused_computation.49 | convolution fusion | flops 20132659200 | bytes 45875200 | tf_op jit(solution)/shard_map/dot_general | solution.py:28
  244.8 0.0 copy-start.1
  244.8 0.0 reduce-scatter.2.cloned.1.call-update
  244.8 0.7 copy-done.1
  245.5 0.1 reshape.68
  245.6 0.1 reshape.58
  245.7 0.3 convolution_bitcast_fusion.1
  245.9 0.2 convolution_bitcast_fusion
  246.2 0.2 fusion.2
  246.4 3.8 convolution_reduce_fusion
  250.2 18.2 %psum.7 = f32[1280]{0:T(1024)} all-reduce(f32[1280]{0:T(1024)S(1)} %convolution_reduce_fusion), channel_id=1, replica_groups=mesh['arc'=8,'col'=4] {'arc'}, use_global_device_ids=true, to_apply=%region_3.4 | all-reduce | flops 1280 | bytes 10240 | tf_op jit(solution)/shard_map/psum | solution.py:55
  268.4 234.1 %reduce-scatter.2.cloned.1.call-done = f32[640,1280]{1,0:T(8,128)} async-done(((f32[5120,1280]{1,0:T(8,128)}), f32[640,1280]{1,0:T(8,128)}) %reduce-scatter.2.cloned.1.call-update) | async-done | bytes 3276816 | tf_op jit(solution)/shard_map/reduce_scatter | solution.py:52
  (6 shorter events, 0.1 us)
Async XLA Ops:
  7.2 189.9 %all-gather.2.cloned.1.call-start = ((), (), s32[]{:S(2)}) async-start(), calls=%async_computation.1 | async-start | bytes 19660800 | tf_op jit(solution)/shard_map/all_gather | solution.py:51
  32.0 5.3 %copy-start = (bf16[1536,1280]{1,0:T(8,128)(2,1)S(1)}, bf16[1536,1280]{1,0:T(8,128)(2,1)}, u32[]{:S(2)}) copy-start(bf16[1536,1280]{1,0:T(8,128)(2,1)} %param.5) | copy-start | bytes 11796484
  45.6 457.0 %reduce-scatter.2.cloned.1.call-start = ((), (), s32[]{:S(2)}) async-start(), calls=%async_computation.2 | async-start | bytes 29491200 | tf_op jit(solution)/shard_map/reduce_scatter | solution.py:52
  244.8 0.7 copy-start.1
Sparse Core Ops, SparseCore 0:
  45.7 151.2 all-gather.1
  245.0 257.5 reduce-scatter.1
